TPU v7x, 256 devices: a whole 4x4x8 slice. The times are simulated.
256 devices in a mesh: group: 4 (over y), shard: 64 (over x, z, core).
Axes of the slice: x: 4, y: 4, z: 8, core: 2. Of those that a mesh axis runs over, the one named last changes fastest.
Arguments:
- activations: bfloat16 [4, 128, 256, 1024], P('group', 'shard'), may hold values from -7 to 7
- out_grad: bfloat16 [4, 128, 256, 1024], P('group', None, 'shard'), may hold values from -1.5 to 1.5
- embedding: bfloat16 [512, 1024], replicated, may hold values from -6 to 6
- counts: int32 [4, 8], P('group'), may hold values from 0 to 256, as said below
- offsets: int32 [4, 8], P('group'), may hold values from 0 to 8, as said below
- layout: int32 [4, 256], P('group'), may hold values from 0 to 511
Outputs:
- input_grad: bfloat16 [4, 128, 256, 1024], P('group', 'shard')
- embedding_grad: float32 [512, 1024], P('group')
Inputs may be any that keep to these rules, and one draw needn't show every extreme that they name: `counts`: A used session slot holds 19 to 256 electrodes; slots after the used ones hold 0. `offsets`: used session slots come first; the first starts at block 0 and each next one where the previous ends, a session taking ceil(count / 32) blocks, all sessions together exactly 8 blocks; unused slots hold 8.
All inputs are finite; a program needn't handle non-finite values.
Results may differ from a plain program's by a relative error of at most 0.012.
The roundings to bfloat16 on the way count: a program that leaves them out, or rounds other values in their place, can miss the bound.
Values may be sent and summed in bfloat16 or wider, within the bound.
A program may use at most 64 MiB of HBM per device.

v0:
```python
import math

import jax
import jax.numpy as jnp
from jax import lax
from jax.sharding import PartitionSpec as P

HEADS = 16
BLOCK = 32


def product(form, left, right):
    return jnp.einsum(form, left, right, preferred_element_type=jnp.float32)


def attend(values, allowed):
    length = values.shape[0]
    head_split = values.reshape(length, HEADS, -1)
    score_scale = 0.5 / math.sqrt(head_split.shape[-1])
    scores = product("qhd,khd->hqk", head_split, head_split) * score_scale
    scores = jnp.where(allowed[None], scores, -1e30)
    row_max = jnp.max(scores, axis=-1, keepdims=True)
    exponent = jnp.exp(scores - row_max)
    weights = (exponent / jnp.sum(exponent, axis=-1, keepdims=True)).astype(jnp.bfloat16)
    attended = product("hqk,khd->qhd", weights, head_split)
    return (head_split, weights, attended)


def attend_back(values, allowed, cotangent):
    head_split, weights, attended = attend(values, allowed)
    length = values.shape[0]
    score_scale = 0.5 / math.sqrt(head_split.shape[-1])
    grad_heads = cotangent.reshape(length, HEADS, -1)
    row_delta = jnp.sum(grad_heads.astype(jnp.float32) * attended, axis=-1)
    grad_weights = product("qhd,khd->hqk", grad_heads, head_split)
    grad_scores = (
        weights.astype(jnp.float32) * (grad_weights - jnp.transpose(row_delta)[:, :, None])
    ).astype(jnp.bfloat16)
    grad_values = score_scale * (
        product("hqk,khd->qhd", grad_scores, head_split)
        + product("hqk,qhd->khd", grad_scores, head_split)
    )
    grad_values = grad_values + product("hqk,qhd->khd", weights, grad_heads)
    return grad_values.reshape(length, -1)


def session_pairs(counts, offsets, electrodes):
    slot_index = jnp.arange(electrodes, dtype=jnp.int32)
    block_index = slot_index // BLOCK
    member = (offsets[None, :] <= block_index[:, None]).astype(jnp.int32)
    session = jnp.sum(member, axis=1) - 1
    chosen = (jnp.arange(offsets.shape[0], dtype=jnp.int32)[None, :] == session[:, None]).astype(
        jnp.int32
    )
    first_slot = jnp.sum(chosen * offsets[None, :], axis=1) * BLOCK
    live_count = jnp.sum(chosen * counts[None, :], axis=1)
    is_live = slot_index - first_slot < live_count
    return (session[:, None] == session[None, :]) & is_live[None, :]


def body(activations, out_grad, embedding, counts, offsets, layout):
    local_in = activations[0]
    electrodes = local_in.shape[1]
    templates = embedding.shape[0]
    allowed = session_pairs(counts[0], offsets[0], electrodes)
    onehot = (layout[0][:, None] == jnp.arange(templates, dtype=jnp.int32)[None, :]).astype(
        jnp.bfloat16
    )
    layout_rows = jnp.dot(onehot, embedding, preferred_element_type=jnp.float32)
    embedded = (local_in.astype(jnp.float32) + layout_rows[None]).astype(jnp.bfloat16)

    def spatial(values):
        return (
            values.astype(jnp.float32) + attend(values, allowed)[2].reshape(electrodes, -1)
        ).astype(jnp.bfloat16)

    mixed = lax.map(spatial, embedded)
    gathered = lax.all_to_all(mixed[None], "shard", split_axis=2, concat_axis=1, tiled=True)
    patches = gathered.shape[1]
    full_mask = jnp.ones((patches, patches), dtype=bool)

    def temporal(couple):
        values, cotangent = couple
        return (cotangent.astype(jnp.float32) + attend_back(values, full_mask, cotangent)).astype(
            jnp.bfloat16
        )

    mixed_grad = lax.map(
        temporal, (jnp.moveaxis(gathered[0], 1, 0), jnp.moveaxis(out_grad[0], 1, 0))
    )
    returned = lax.all_to_all(
        jnp.moveaxis(mixed_grad, 0, 1)[None], "shard", split_axis=1, concat_axis=2, tiled=True
    )

    def spatial_back(couple):
        values, cotangent = couple
        return cotangent.astype(jnp.float32) + attend_back(values, allowed, cotangent)

    full_grad = lax.map(spatial_back, (embedded, returned[0]))
    input_grad = full_grad.astype(jnp.bfloat16)[None]
    electrode_grad = jnp.sum(full_grad, axis=0)
    spread = jnp.transpose(onehot.astype(jnp.float32))
    own_rows = templates // lax.axis_size("group")
    local_table = jnp.dot(spread, electrode_grad, precision=lax.Precision.HIGHEST)
    summed_table = lax.psum(local_table, ("group", "shard"))
    table_grad = lax.dynamic_slice_in_dim(
        summed_table, lax.axis_index("group") * own_rows, own_rows, 0
    )
    return (input_grad, table_grad)


def solution(mesh):
    placed = (
        P("group", "shard", None, None),
        P("group", None, "shard", None),
        P(),
        P("group", None),
        P("group", None),
        P("group", None),
    )
    return jax.shard_map(
        body,
        mesh=mesh,
        in_specs=placed,
        out_specs=(P("group", "shard", None, None), P("group", None)),
        check_vma=False,
    )
```

profile of v0, /device:TPU:1, one launch (start us, length us, event | category | flops | bytes accessed | tf_op | source)
XLA Modules:
  0.0 439.5 jit_solution(2112430780743667618)
XLA Ops:
  8.1 1.5 copy.79
  10.5 14.4 %while.33 = (s32[]{:T(128)}, bf16[2,256,1024]{1,2,0:T(8,128)(2,1)}, bf16[2,256,1024]{1,2,0:T(8,128)(2,1)S(1)}, s32[256]{0:T(256)S(1)}, pred[256]{0:T(512)(128)(4,1)S(1)}, /*index=5*/s32[]{:T(128)}) while((s32[]{:T(128)}, bf16[2,256,1024]{1,2,0:T(8,128)(2,1)}, bf16[2,256,1024]{1,2,0:T(8,128)(2,1)S(1)}, s32[256]{0:T(256)S(1)}, ...), condition=%wide.region_6.7_spmd.clone, body=%wide.region_3.6_spmd.clone.sunk | while | flops 275644672 | bytes 13797193 | solution.py:77
  10.7 3.4 fusion.141
  14.2 2.7 fusion.142
  16.8 0.9 constant_dynamic-update-slice_fusion.7
  18.0 3.4 fusion.141
  21.4 2.7 fusion.142
  24.0 0.9 constant_dynamic-update-slice_fusion.7
  25.0 3.7 copy.81
  28.7 13.0 %all-to-all-start = ((bf16[1,2,256,1024]{3,1,0,2:T(2,128)(2,1)}), bf16[1,2,256,1024]{3,1,0,2:T(2,128)(2,1)S(1)}, u32[]{:S(2)}, u32[]{:S(2)}) async-start(bf16[1,2,256,1024]{3,1,0,2:T(2,128)(2,1)} %bitcast.188), calls=%async_computation | async-start | bytes 2097152 | tf_op jit(solution)/shard_map/all_to_all | solution.py:78
  41.7 2.7 copy.78
  44.4 25.8 %all-to-all-done = bf16[1,2,256,1024]{3,1,0,2:T(2,128)(2,1)S(1)} async-done(((bf16[1,2,256,1024]{3,1,0,2:T(2,128)(2,1)}), bf16[1,2,256,1024]{3,1,0,2:T(2,128)(2,1)S(1)}, u32[]{:S(2)}, u32[]{:S(2)}) %all-to-all-start) | async-done | bytes 1048608 | tf_op jit(solution)/shard_map/all_to_all | solution.py:78
  70.2 1.5 copy.82
  71.7 2.7 copy.83
  74.4 26.1 %while.32 = (s32[]{:T(128)}, bf16[4,128,1024]{1,2,0:T(8,128)(2,1)}, bf16[4,128,1024]{1,2,0:T(8,128)(2,1)}, bf16[4,128,1024]{1,2,0:T(8,128)(2,1)}, s32[]{:T(128)}) while((s32[]{:T(128)}, bf16[4,128,1024]{1,2,0:T(8,128)(2,1)}, bf16[4,128,1024]{1,2,0:T(8,128)(2,1)}, bf16[4,128,1024]{1,2,0:T(8,128)(2,1)}, s32[]{:T(128)}) %tuple.88), condition=%wide.region_11.12_spmd, body=%wide.region_7.11_spmd.sunk | while | flops 204863616 | bytes 12616257 | solution.py:88
  74.4 1.1 constant_dynamic-slice_fusion.9
  75.5 1.5 fusion.133
  77.0 1.3 divide_convert_fusion.7
  81.0 1.1 constant_dynamic-slice_fusion.9
  82.0 1.5 fusion.133
  83.5 1.3 divide_convert_fusion.7
  87.5 1.1 constant_dynamic-slice_fusion.9
  88.5 1.5 fusion.133
  90.0 1.3 divide_convert_fusion.7
  94.0 1.1 constant_dynamic-slice_fusion.9
  95.1 1.5 fusion.133
  96.5 1.3 divide_convert_fusion.7
  100.5 2.7 copy.84
  103.2 6.2 %all-to-all-start.1 = ((bf16[1,128,4,1024]{3,2,0,1:T(4,128)(2,1)}), bf16[1,128,4,1024]{3,2,0,1:T(4,128)(2,1)S(1)}, u32[]{:S(2)}, u32[]{:S(2)}) async-start(bf16[1,128,4,1024]{3,2,0,1:T(4,128)(2,1)} %bitcast.187), calls=%async_computation.1 | async-start | bytes 2097152 | tf_op jit(solution)/shard_map/all_to_all | solution.py:91
  109.7 28.3 %all-to-all-done.1 = bf16[1,128,4,1024]{3,2,0,1:T(4,128)(2,1)S(1)} async-done(((bf16[1,128,4,1024]{3,2,0,1:T(4,128)(2,1)}), bf16[1,128,4,1024]{3,2,0,1:T(4,128)(2,1)S(1)}, u32[]{:S(2)}, u32[]{:S(2)}) %all-to-all-start.1) | async-done | bytes 1048608 | tf_op jit(solution)/shard_map/all_to_all | solution.py:91
  137.9 2.1 copy.85
  140.0 3.6 copy.86
  143.6 23.5 %while.34 = (s32[]{:T(128)}, f32[2,256,1024]{1,2,0:T(8,128)}, bf16[2,256,1024]{1,2,0:T(8,128)(2,1)}, bf16[2,256,1024]{1,2,0:T(8,128)(2,1)S(1)}, s32[256]{0:T(256)S(1)}, /*index=5*/pred[256]{0:T(512)(128)(4,1)S(1)}, s32[]{:T(128)}) while((s32[]{:T(128)}, f32[2,256,1024]{1,2,0:T(8,128)}, bf16[2,256,1024]{1,2,0:T(8,128)(2,1)}, ...), condition=%wide.region_16.17_spmd.clone, body=%wide.region_12.16_spmd.clone.sunk | while | flops 818016512 | bytes 37422928 | solution.py:99
  143.6 1.1 constant_dynamic-slice_fusion.11
  144.9 3.4 fusion.155
  148.3 2.6 divide_convert_fusion.9
  151.4 0.8 multiply_convert_fusion.2
  154.3 1.1 constant_dynamic-update-slice_fusion.8
  155.4 1.1 constant_dynamic-slice_fusion.11
  156.6 3.4 fusion.155
  160.1 2.6 divide_convert_fusion.9
  163.2 0.8 multiply_convert_fusion.2
  166.0 1.1 constant_dynamic-update-slice_fusion.8
  167.2 1.8 reduce_sum.84
  169.0 2.5 fusion.41
  171.6 2.5 copy.87
  174.1 256.7 %all-reduce.2.cloned.1.call-done = f32[512,1024]{1,0:T(8,128)} async-done(((f32[512,1024]{1,0:T(8,128)}), f32[512,1024]{1,0:T(8,128)}) %all-reduce.2.cloned.1.call-update) | async-done | bytes 2097168 | tf_op jit(solution)/shard_map/psum | solution.py:105
  430.8 1.9 constant_dynamic-slice_fusion.5
  (58 shorter events, 18.1 us)
Async XLA Ops:
  7.2 2.5 copy-start
  7.2 2.4 copy-start.2
  7.2 2.4 copy-start.3
  7.2 2.5 copy-start.1
  28.7 41.5 %all-to-all-start = ((bf16[1,2,256,1024]{3,1,0,2:T(2,128)(2,1)}), bf16[1,2,256,1024]{3,1,0,2:T(2,128)(2,1)S(1)}, u32[]{:S(2)}, u32[]{:S(2)}) async-start(bf16[1,2,256,1024]{3,1,0,2:T(2,128)(2,1)} %bitcast.188), calls=%async_computation | async-start | bytes 2097152 | tf_op jit(solution)/shard_map/all_to_all | solution.py:78
  103.2 34.7 %all-to-all-start.1 = ((bf16[1,128,4,1024]{3,2,0,1:T(4,128)(2,1)}), bf16[1,128,4,1024]{3,2,0,1:T(4,128)(2,1)S(1)}, u32[]{:S(2)}, u32[]{:S(2)}) async-start(bf16[1,128,4,1024]{3,2,0,1:T(4,128)(2,1)} %bitcast.187), calls=%async_computation.1 | async-start | bytes 2097152 | tf_op jit(solution)/shard_map/all_to_all | solution.py:91
  109.4 321.4 %all-reduce.2.cloned.1.call-start = ((), (), s32[]{:S(2)}) async-start(), calls=%async_computation.2 | async-start | bytes 4194304 | tf_op jit(solution)/shard_map/psum | solution.py:105
Sparse Core Ops, SparseCore 0:
  171.7 259.0 all-reduce.1
where the time goes:
time: 441 us; the launch traced here: 440 us
  waiting for transfers between devices  311 us (71%)
  matrix products  42.1 us (10%)
  local copies, waits for them, and re-layouts  31.5 us (7%)
  other arithmetic  21.3 us (5%)
  starting transfers between devices  19.4 us (4%)
  between operations  14.2 us (3%)
    psum x1, waiting for transfers between devices, body(): summed_table = lax.psum(local_table, ('group', 'shard'))  257 us
    all_to_all x1, waiting for transfers between devices, body(): lax.all_to_all(jnp.moveaxis(mixed_grad, 0, 1)[None], 'shard', split_axis=...  28.3 us
    all_to_all x1, waiting for transfers between devices, body(): lax.all_to_all(mixed[None], 'shard', split_axis=2, concat_axis=1, tiled=T...  25.8 us
    sub x8, matrix products, attend(): exponent = jnp.exp(scores - row_max)  19.6 us
    dot_general x32, matrix products, product(): return jnp.einsum(form, left, right, preferred_element_type=jnp.float32)  19.4 us
    all_to_all x1, starting transfers between devices, body(): lax.all_to_all(mixed[None], 'shard', split_axis=2, concat_axis=1, tiled=T...  13 us
    convert_element_type x6, other arithmetic, attend(): (exponent / jnp.sum(exponent, axis=-1, keepdims=True)).astype(jnp.bfloat16)  10.6 us
  transfers between devices with their start and end apart: 3, of which 3 were waited for; matrix products, arithmetic and copies ran while one was open for 1% of the time, Pallas kernels for 0%

commit v1 on v0

--- a/solution.py
+++ b/solution.py
@@ -99,13 +99,24 @@
     full_grad = lax.map(spatial_back, (embedded, returned[0]))
     input_grad = full_grad.astype(jnp.bfloat16)[None]
     electrode_grad = jnp.sum(full_grad, axis=0)
-    spread = jnp.transpose(onehot.astype(jnp.float32))
-    own_rows = templates // lax.axis_size("group")
-    local_table = jnp.dot(spread, electrode_grad, precision=lax.Precision.HIGHEST)
-    summed_table = lax.psum(local_table, ("group", "shard"))
-    table_grad = lax.dynamic_slice_in_dim(
-        summed_table, lax.axis_index("group") * own_rows, own_rows, 0
+    shards = lax.axis_size("shard")
+    groups = lax.axis_size("group")
+    width = local_in.shape[2]
+    pieces = jnp.transpose(electrode_grad).astype(jnp.bfloat16)
+    pieces = pieces.reshape(shards, width // shards, electrodes)
+    arrived = lax.all_to_all(pieces, "shard", split_axis=0, concat_axis=0, tiled=True)
+    own_columns = jnp.sum(arrived.astype(jnp.float32), axis=0)
+    column_table = jnp.dot(
+        own_columns.astype(jnp.bfloat16), onehot, preferred_element_type=jnp.float32
     )
+    own_rows = templates // groups
+    column_table = column_table.reshape(width // shards, groups, own_rows)
+    from_groups = lax.all_to_all(
+        jnp.moveaxis(column_table, 1, 0), "group", split_axis=0, concat_axis=0, tiled=True
+    )
+    own_part = jnp.sum(from_groups, axis=0)
+    gathered_table = lax.all_gather(own_part, "shard", axis=0, tiled=True)
+    table_grad = jnp.transpose(gathered_table)
     return (input_grad, table_grad)
 
 

time: 441 us -> 251 us (0.57)
  waiting for transfers between devices: 311 us -> 73.4 us
  blocking collectives: 0 us -> 51.2 us
  between operations: 14.2 us -> 0.74 us
  starting transfers between devices: 19.4 us -> 29.5 us
    psum x1 -> x0, waiting for transfers between devices: 257 us -> none  [body(): summed_table = lax.psum(local_table, ('group', 'shard'))]
    all_gather x0 -> x1, blocking collectives: none -> 51.2 us  [body(): gathered_table = lax.all_gather(own_part, 'shard', axis=0, tiled=True)]
    all_to_all x0 -> x2, waiting for transfers between devices: none -> 19 us  [the longest x1 17.3 us: body(): lax.all_to_all(pieces, 'shard', split_axis=0, concat_axis=0, tiled=True)]
    all_to_all x0 -> x2, starting transfers between devices: none -> 10.4 us  [the longest x1 6.19 us: body(): lax.all_to_all(pieces, 'shard', split_axis=0, concat_axis=0, tiled=True)]
  transfers between devices with their start and end apart: 3 -> 4, of which waited for: 3 -> 4; matrix products, arithmetic and copies ran while one was open for 1% -> 2% of each run, Pallas kernels for 0% -> 0%
where the time goes in v1:
time: 251 us; the launch traced here: 250 us
  waiting for transfers between devices  73.4 us (29%)
  blocking collectives  51.2 us (20%)
  matrix products  41.2 us (16%)
  local copies, waits for them, and re-layouts  30.6 us (12%)
  starting transfers between devices  29.5 us (12%)
  other arithmetic  22.9 us (9%)
    all_gather x1, blocking collectives, body(): gathered_table = lax.all_gather(own_part, 'shard', axis=0, tiled=True)  51.2 us
    all_to_all x1, waiting for transfers between devices, body(): lax.all_to_all(jnp.moveaxis(mixed_grad, 0, 1)[None], 'shard', split_axis=...  28.5 us
    all_to_all x1, waiting for transfers between devices, body(): lax.all_to_all(mixed[None], 'shard', split_axis=2, concat_axis=1, tiled=T...  25.8 us
    sub x8, matrix products, attend(): exponent = jnp.exp(scores - row_max)  19.6 us
    dot_general x32, matrix products, product(): return jnp.einsum(form, left, right, preferred_element_type=jnp.float32)  19.4 us
    all_to_all x1, waiting for transfers between devices, body(): lax.all_to_all(pieces, 'shard', split_axis=0, concat_axis=0, tiled=True)  17.3 us
    all_to_all x1, starting transfers between devices, body(): lax.all_to_all(mixed[None], 'shard', split_axis=2, concat_axis=1, tiled=T...  13 us
    convert_element_type x6, other arithmetic, attend(): (exponent / jnp.sum(exponent, axis=-1, keepdims=True)).astype(jnp.bfloat16)  10.6 us
  transfers between devices with their start and end apart: 4, of which 4 were waited for; matrix products, arithmetic and copies ran while one was open for 2% of the time, Pallas kernels for 0%

profile of v1, /device:TPU:1, one launch (start us, length us, event | category | flops | bytes accessed | tf_op | source)
XLA Modules:
  0.0 249.8 jit_solution(14660771344484138781)
XLA Ops:
  1.5 1.5 copy.80
  3.8 1.3 fusion.39
  5.3 14.4 %while.33 = (s32[]{:T(128)}, bf16[2,256,1024]{1,2,0:T(8,128)(2,1)}, bf16[2,256,1024]{1,2,0:T(8,128)(2,1)S(1)}, s32[256]{0:T(256)S(1)}, pred[256]{0:T(512)(128)(4,1)S(1)}, /*index=5*/s32[]{:T(128)}) while((s32[]{:T(128)}, bf16[2,256,1024]{1,2,0:T(8,128)(2,1)}, bf16[2,256,1024]{1,2,0:T(8,128)(2,1)S(1)}, s32[256]{0:T(256)S(1)}, ...), condition=%wide.region_6.7_spmd.clone, body=%wide.region_3.6_spmd.clone.sunk | while | flops 275644672 | bytes 13797193 | solution.py:77
  5.5 3.4 %fusion.140 = (f32[16,256]{1,0:T(8,128)S(1)}, f32[16,256,256]{1,2,0:T(8,128)}) fusion(pred[256,256]{0,1:T(8,128)(4,1)S(1)} %compare_and_fusion.4, bf16[256,16,64]{0,2,1:T(8,128)(2,1)S(1)} %bitcast.190), kind=kOutput, calls=%fused_computation.86.clone.1 | convolution fusion | flops 138412288 | bytes 4800512 | tf_op jit(solution)/shard_map/while/body/eval_jaxpr/sub | solution.py:23
  8.9 2.7 %fusion.141 = f32[16,64,256]{2,1,0:T(8,128)S(1)} fusion(bf16[256,16,64]{0,2,1:T(8,128)(2,1)S(1)} %bitcast.191, f32[16,256,256]{1,2,0:T(8,128)} %get-tuple-element.283, f32[16,256]{1,0:T(8,128)S(1)} %get-tuple-element.284), kind=kOutput, calls=%fused_computation.30.clone.1 | convolution fusion | flops 136314880 | bytes 5783552 | tf_op jit(solution)/shard_map/while/body/eval_jaxpr/hqk,khd->qhd/dot_general | solution.py:13
  12.7 3.4 %fusion.140 = (f32[16,256]{1,0:T(8,128)S(1)}, f32[16,256,256]{1,2,0:T(8,128)}) fusion(pred[256,256]{0,1:T(8,128)(4,1)S(1)} %compare_and_fusion.4, bf16[256,16,64]{0,2,1:T(8,128)(2,1)S(1)} %bitcast.190), kind=kOutput, calls=%fused_computation.86.clone.1 | convolution fusion | flops 138412288 | bytes 4800512 | tf_op jit(solution)/shard_map/while/body/eval_jaxpr/sub | solution.py:23
  16.1 2.7 %fusion.141 = f32[16,64,256]{2,1,0:T(8,128)S(1)} fusion(bf16[256,16,64]{0,2,1:T(8,128)(2,1)S(1)} %bitcast.191, f32[16,256,256]{1,2,0:T(8,128)} %get-tuple-element.283, f32[16,256]{1,0:T(8,128)S(1)} %get-tuple-element.284), kind=kOutput, calls=%fused_computation.30.clone.1 | convolution fusion | flops 136314880 | bytes 5783552 | tf_op jit(solution)/shard_map/while/body/eval_jaxpr/hqk,khd->qhd/dot_general | solution.py:13
  19.7 3.7 %copy.82 = bf16[2,256,1024]{2,0,1:T(2,128)(2,1)} copy(bf16[2,256,1024]{1,2,0:T(8,128)(2,1)} %get-tuple-element.73) | data formatting | bytes 2097152 | tf_op jit(solution)/shard_map/while | solution.py:77
  23.5 13.0 %all-to-all-start = ((bf16[1,2,256,1024]{3,1,0,2:T(2,128)(2,1)}), bf16[1,2,256,1024]{3,1,0,2:T(2,128)(2,1)S(1)}, u32[]{:S(2)}, u32[]{:S(2)}) async-start(bf16[1,2,256,1024]{3,1,0,2:T(2,128)(2,1)} %bitcast.195), calls=%async_computation | async-start | bytes 2097152 | tf_op jit(solution)/shard_map/all_to_all | solution.py:78
  36.5 2.7 %copy.79 = bf16[1,128,4,1024]{1,3,2,0:T(8,128)(2,1)} copy(bf16[1,128,4,1024]{3,2,1,0:T(4,128)(2,1)} %param.13) | data formatting | bytes 2097152 | tf_op args[1]
  39.1 25.8 %all-to-all-done = bf16[1,2,256,1024]{3,1,0,2:T(2,128)(2,1)S(1)} async-done(((bf16[1,2,256,1024]{3,1,0,2:T(2,128)(2,1)}), bf16[1,2,256,1024]{3,1,0,2:T(2,128)(2,1)S(1)}, u32[]{:S(2)}, u32[]{:S(2)}) %all-to-all-start) | async-done | bytes 1048608 | tf_op jit(solution)/shard_map/all_to_all | solution.py:78
  65.0 1.5 copy.83
  66.5 2.7 %copy.84 = bf16[4,128,1024]{1,2,0:T(8,128)(2,1)} copy(bf16[4,128,1024]{2,0,1:T(4,128)(2,1)} %bitcast.197) | data formatting | bytes 2097152 | tf_op jit(solution)/shard_map/while | solution.py:88
  69.2 26.1 %while.32 = (s32[]{:T(128)}, bf16[4,128,1024]{1,2,0:T(8,128)(2,1)}, bf16[4,128,1024]{1,2,0:T(8,128)(2,1)}, bf16[4,128,1024]{1,2,0:T(8,128)(2,1)}, s32[]{:T(128)}) while((s32[]{:T(128)}, bf16[4,128,1024]{1,2,0:T(8,128)(2,1)}, bf16[4,128,1024]{1,2,0:T(8,128)(2,1)}, bf16[4,128,1024]{1,2,0:T(8,128)(2,1)}, s32[]{:T(128)}) %tuple.88), condition=%wide.region_11.12_spmd, body=%wide.region_7.11_spmd.sunk | while | flops 204863616 | bytes 12616257 | solution.py:88
  69.2 1.1 constant_dynamic-slice_fusion.8
  70.3 1.5 fusion.132
  71.7 1.3 divide_convert_fusion.7
  75.7 1.1 constant_dynamic-slice_fusion.8
  76.8 1.5 fusion.132
  78.3 1.3 divide_convert_fusion.7
  82.2 1.1 constant_dynamic-slice_fusion.8
  83.3 1.5 fusion.132
  84.8 1.3 divide_convert_fusion.7
  88.7 1.1 constant_dynamic-slice_fusion.8
  89.8 1.5 fusion.132
  91.3 1.3 divide_convert_fusion.7
  95.3 2.7 %copy.85 = bf16[4,128,1024]{2,0,1:T(4,128)(2,1)} copy(bf16[4,128,1024]{1,2,0:T(8,128)(2,1)} %get-tuple-element.74) | data formatting | bytes 2097152 | tf_op jit(solution)/shard_map/while | solution.py:88
  98.0 6.2 %all-to-all-start.1 = ((bf16[1,128,4,1024]{3,2,0,1:T(4,128)(2,1)}), bf16[1,128,4,1024]{3,2,0,1:T(4,128)(2,1)S(1)}, u32[]{:S(2)}, u32[]{:S(2)}) async-start(bf16[1,128,4,1024]{3,2,0,1:T(4,128)(2,1)} %bitcast.196), calls=%async_computation.1 | async-start | bytes 2097152 | tf_op jit(solution)/shard_map/all_to_all | solution.py:91
  104.2 28.5 %all-to-all-done.1 = bf16[1,128,4,1024]{3,2,0,1:T(4,128)(2,1)S(1)} async-done(((bf16[1,128,4,1024]{3,2,0,1:T(4,128)(2,1)}), bf16[1,128,4,1024]{3,2,0,1:T(4,128)(2,1)S(1)}, u32[]{:S(2)}, u32[]{:S(2)}) %all-to-all-start.1) | async-done | bytes 1048608 | tf_op jit(solution)/shard_map/all_to_all | solution.py:91
  132.7 2.1 copy.86
  134.8 3.6 %copy.87 = bf16[2,256,1024]{1,2,0:T(8,128)(2,1)} copy(bf16[2,256,1024]{2,0,1:T(2,128)(2,1)} %bitcast.198) | data formatting | bytes 2097152
  138.4 23.5 %while.34 = (s32[]{:T(128)}, f32[2,256,1024]{1,2,0:T(8,128)}, bf16[2,256,1024]{1,2,0:T(8,128)(2,1)}, bf16[2,256,1024]{1,2,0:T(8,128)(2,1)S(1)}, s32[256]{0:T(256)S(1)}, /*index=5*/pred[256]{0:T(512)(128)(4,1)S(1)}, s32[]{:T(128)}) while((s32[]{:T(128)}, f32[2,256,1024]{1,2,0:T(8,128)}, bf16[2,256,1024]{1,2,0:T(8,128)(2,1)}, ...), condition=%wide.region_16.17_spmd.clone, body=%wide.region_12.16_spmd.clone.sunk | while | flops 818016512 | bytes 37422928 | solution.py:99
  138.4 1.1 constant_dynamic-slice_fusion.10
  139.6 3.4 %fusion.154 = (f32[16,256]{1,0:T(8,128)S(1)}, f32[16,256,256]{1,2,0:T(8,128)}) fusion(pred[256,256]{0,1:T(8,128)(4,1)S(1)} %compare_and_fusion.5, bf16[256,16,64]{0,2,1:T(8,128)(2,1)S(1)} %bitcast.174), kind=kOutput, calls=%fused_computation.87.clone.1 | convolution fusion | flops 138412288 | bytes 4800512 | tf_op jit(solution)/shard_map/while/body/eval_jaxpr/sub | solution.py:23
  143.1 2.6 %divide_convert_fusion.9 = bf16[16,256,256]{1,2,0:T(8,128)(2,1)S(1)} fusion(f32[16,256,256]{1,2,0:T(8,128)} %get-tuple-element.292, f32[16,256]{1,0:T(8,128)S(1)} %get-tuple-element.293), kind=kLoop, calls=%fused_computation.42.clone.1 | loop fusion | flops 2097152 | bytes 6307840 | tf_op jit(solution)/shard_map/while/body/eval_jaxpr/convert_element_type | solution.py:24
  149.0 1.1 constant_dynamic-update-slice_fusion.8
  150.1 1.1 constant_dynamic-slice_fusion.10
  151.4 3.4 %fusion.154 = (f32[16,256]{1,0:T(8,128)S(1)}, f32[16,256,256]{1,2,0:T(8,128)}) fusion(pred[256,256]{0,1:T(8,128)(4,1)S(1)} %compare_and_fusion.5, bf16[256,16,64]{0,2,1:T(8,128)(2,1)S(1)} %bitcast.174), kind=kOutput, calls=%fused_computation.87.clone.1 | convolution fusion | flops 138412288 | bytes 4800512 | tf_op jit(solution)/shard_map/while/body/eval_jaxpr/sub | solution.py:23
  154.8 2.6 %divide_convert_fusion.9 = bf16[16,256,256]{1,2,0:T(8,128)(2,1)S(1)} fusion(f32[16,256,256]{1,2,0:T(8,128)} %get-tuple-element.292, f32[16,256]{1,0:T(8,128)S(1)} %get-tuple-element.293), kind=kLoop, calls=%fused_computation.42.clone.1 | loop fusion | flops 2097152 | bytes 6307840 | tf_op jit(solution)/shard_map/while/body/eval_jaxpr/convert_element_type | solution.py:24
  160.8 1.1 constant_dynamic-update-slice_fusion.8
  161.9 2.7 %reduce_sum.105 = bf16[256,1024]{0,1:T(8,128)(2,1)} reduce(f32[2,256,1024]{1,2,0:T(8,128)} %get-tuple-element.75, f32[]{:T(128)} %constant.80.clone.1), dimensions={0}, to_apply=%region_17.18 | reduce | flops 262144 | bytes 2621444 | tf_op jit(solution)/shard_map/reduce_sum | solution.py:101
  164.6 6.2 %all-to-all-start.2 = ((bf16[64,16,256]{2,1,0:T(8,128)(2,1)}), bf16[64,16,256]{2,1,0:T(8,128)(2,1)S(1)}, u32[]{:S(2)}, u32[]{:S(2)}) async-start(bf16[64,16,256]{2,1,0:T(8,128)(2,1)} %bitcast.24), calls=%async_computation.2 | async-start | bytes 1048576 | tf_op jit(solution)/shard_map/all_to_all | solution.py:107
  170.8 17.3 %all-to-all-done.2 = bf16[64,16,256]{2,1,0:T(8,128)(2,1)S(1)} async-done(((bf16[64,16,256]{2,1,0:T(8,128)(2,1)}), bf16[64,16,256]{2,1,0:T(8,128)(2,1)S(1)}, u32[]{:S(2)}, u32[]{:S(2)}) %all-to-all-start.2) | async-done | bytes 524320 | tf_op jit(solution)/shard_map/all_to_all | solution.py:107
  189.1 4.2 %all-to-all-start.3 = ((f32[4,16,128]{2,1,0:T(8,128)}), f32[4,16,128]{2,1,0:T(8,128)S(1)}, u32[]{:S(2)}, u32[]{:S(2)}) async-start(f32[4,16,128]{2,1,0:T(8,128)} %convolution_bitcast_fusion.2), calls=%async_computation.3 | async-start | bytes 65536 | tf_op jit(solution)/shard_map/all_to_all | solution.py:114
  193.3 2.5 %copy.88 = bf16[2,256,1024]{2,1,0:T(8,128)(2,1)} copy(f32[2,256,1024]{1,2,0:T(8,128)} %get-tuple-element.75) | data formatting | bytes 3145728 | tf_op jit(solution)/shard_map/while | solution.py:99
  195.8 1.8 all-to-all-done.3
  197.6 51.2 %all_gather.3 = f32[1024,128]{1,0:T(8,128)S(1)} all-gather(f32[16,128]{1,0:T(8,128)S(1)} %reduce_sum.107), channel_id=1, replica_groups=mesh['group'=4,'shard'=64] {'shard'}, dimensions={0}, use_global_device_ids=true | all-gather | bytes 532480 | tf_op jit(solution)/shard_map/all_gather | solution.py:118
  248.8 1.0 copy.89
  (59 shorter events, 22.4 us)
Async XLA Ops:
  0.6 3.1 %copy-start = (bf16[512,1024]{1,0:T(8,128)(2,1)S(1)}, bf16[512,1024]{1,0:T(8,128)(2,1)}, u32[]{:S(2)}) copy-start(bf16[512,1024]{1,0:T(8,128)(2,1)} %param.14) | copy-start | bytes 3145732
  23.5 41.5 %all-to-all-start = ((bf16[1,2,256,1024]{3,1,0,2:T(2,128)(2,1)}), bf16[1,2,256,1024]{3,1,0,2:T(2,128)(2,1)S(1)}, u32[]{:S(2)}, u32[]{:S(2)}) async-start(bf16[1,2,256,1024]{3,1,0,2:T(2,128)(2,1)} %bitcast.195), calls=%async_computation | async-start | bytes 2097152 | tf_op jit(solution)/shard_map/all_to_all | solution.py:78
  98.0 34.7 %all-to-all-start.1 = ((bf16[1,128,4,1024]{3,2,0,1:T(4,128)(2,1)}), bf16[1,128,4,1024]{3,2,0,1:T(4,128)(2,1)S(1)}, u32[]{:S(2)}, u32[]{:S(2)}) async-start(bf16[1,128,4,1024]{3,2,0,1:T(4,128)(2,1)} %bitcast.196), calls=%async_computation.1 | async-start | bytes 2097152 | tf_op jit(solution)/shard_map/all_to_all | solution.py:91
  161.9 26.3 %copy-start.1 = (s32[1,256]{1,0:T(1,128)S(1)}, s32[1,256]{1,0:T(1,128)}, u32[]{:S(2)}) copy-start(s32[1,256]{1,0:T(1,128)} %param.17) | copy-start | bytes 3076
  164.6 23.5 %all-to-all-start.2 = ((bf16[64,16,256]{2,1,0:T(8,128)(2,1)}), bf16[64,16,256]{2,1,0:T(8,128)(2,1)S(1)}, u32[]{:S(2)}, u32[]{:S(2)}) async-start(bf16[64,16,256]{2,1,0:T(8,128)(2,1)} %bitcast.24), calls=%async_computation.2 | async-start | bytes 1048576 | tf_op jit(solution)/shard_map/all_to_all | solution.py:107
  189.1 8.5 %all-to-all-start.3 = ((f32[4,16,128]{2,1,0:T(8,128)}), f32[4,16,128]{2,1,0:T(8,128)S(1)}, u32[]{:S(2)}, u32[]{:S(2)}) async-start(f32[4,16,128]{2,1,0:T(8,128)} %convolution_bitcast_fusion.2), calls=%async_computation.3 | async-start | bytes 65536 | tf_op jit(solution)/shard_map/all_to_all | solution.py:114

commit v2 on v0

v2 whole, which is shorter than its diff:
```python
import functools

import jax
import jax.numpy as jnp
from jax import lax
from jax.experimental import pallas as pl
from jax.experimental.pallas import tpu as pltpu
from jax.sharding import PartitionSpec as P

MESH = pl.DeviceIdType.MESH
SHARDS = 64
GROUPS = 4
HALF = 64
LANES = 128
PAIRS = 8
CHUNKS = 4
PER_CHUNK = PAIRS // CHUNKS
SLOTS = 256
PATCHES = 128
TEMPLATES = 512
WIDTH = 1024
OWN_COLS = WIDTH // SHARDS
OWN_ROWS = TEMPLATES // GROUPS
SCALE = 0.0625
BLOCK_SHIFT = 5
SESSIONS = 8
F32 = jnp.float32
BF16 = jnp.bfloat16


def mm(a, b):
    return lax.dot_general(a, b, (((1,), (0,)), ((), ())), preferred_element_type=F32)


def mm_nt(a, b):
    return lax.dot_general(a, b, (((1,), (1,)), ((), ())), preferred_element_type=F32)


def head_masks(values):
    lane = lax.broadcasted_iota(jnp.int32, values.shape, 1)
    zero = jnp.zeros_like(values)
    return jnp.where(lane < HALF, values, zero), jnp.where(lane < HALF, zero, values)


def column_softmax(scores):
    top = jnp.max(scores, axis=0, keepdims=True)
    exponent = jnp.exp(scores - top)
    total = jnp.sum(exponent, axis=0, keepdims=True)
    return (exponent * (1.0 / total)).astype(BF16)


def turned_grad_scores(weights_t, grad_weights_t):
    wide = weights_t.astype(F32)
    row_delta = jnp.sum(wide * grad_weights_t, axis=0, keepdims=True)
    return (wide * (grad_weights_t - row_delta)).astype(BF16)


def spatial_pair(values, bias):
    scaled = values * jnp.asarray(SCALE, BF16)
    values_t = jnp.transpose(values)
    weights, parts = [], []
    for head, masked in enumerate(head_masks(values)):
        scores_t = mm_nt(scaled, masked) + bias
        weights_t = column_softmax(scores_t)
        weights.append(weights_t)
        parts.append(mm(values_t[head * HALF : (head + 1) * HALF], weights_t))
    attended = jnp.transpose(jnp.concatenate(parts, axis=0))
    return values.astype(F32) + attended, weights


def temporal_pair(values, cotangent):
    scaled = values * jnp.asarray(SCALE, BF16)
    scaled_t = jnp.transpose(scaled)
    stacked = jnp.concatenate(head_masks(values), axis=0)
    stacked_grad = jnp.concatenate(head_masks(cotangent), axis=0)
    scores_t = mm_nt(scaled, stacked)
    weights_t = column_softmax(scores_t)
    grad_weights_t = mm_nt(values, stacked_grad)
    grad_scores_t = turned_grad_scores(weights_t, grad_weights_t)
    stacked_scaled = stacked * jnp.asarray(SCALE, BF16)
    direct = mm(grad_scores_t, stacked_scaled) + mm(weights_t, stacked_grad)
    turned = mm(scaled_t, grad_scores_t)
    row = lax.broadcasted_iota(jnp.int32, (LANES, LANES), 0)
    turned = jnp.where(row < HALF, turned[:, :LANES], turned[:, LANES:])
    return cotangent.astype(F32) + direct + jnp.transpose(turned)


def spatial_back_pair(values, weights, cotangent):
    scaled = values * jnp.asarray(SCALE, BF16)
    scaled_t = jnp.transpose(scaled)
    total = cotangent.astype(F32)
    parts = []
    pieces = zip(weights, head_masks(scaled), head_masks(cotangent))
    for head, (weights_t, scaled_head, grad_head) in enumerate(pieces):
        grad_weights_t = mm_nt(values, grad_head)
        grad_scores_t = turned_grad_scores(weights_t, grad_weights_t)
        total = total + (mm(grad_scores_t, scaled_head) + mm(weights_t, grad_head))
        parts.append(mm(scaled_t[head * HALF : (head + 1) * HALF], grad_scores_t))
    return total + jnp.transpose(jnp.concatenate(parts, axis=0))


def weave(first, second, roll):
    columns = first.shape[1]
    first = first.reshape(SLOTS // 8, 8, columns)
    second = second.reshape(SLOTS // 8, 8, columns)
    low = lax.broadcasted_iota(jnp.int32, first.shape, 1) < 4
    even = jnp.where(low, first, roll(second, 4, 1))
    odd = jnp.where(low, roll(first, 4, 1), second)
    return jnp.stack([even, odd], axis=1).reshape(SHARDS, 8, columns)


def unweave(blocks, roll):
    columns = blocks.shape[2]
    blocks = blocks.reshape(SLOTS // 8, 2, 8, columns)
    even, odd = blocks[:, 0], blocks[:, 1]
    low = lax.broadcasted_iota(jnp.int32, even.shape, 1) < 4
    first = jnp.where(low, even, roll(odd, 4, 1))
    second = jnp.where(low, roll(even, 4, 1), odd)
    return first.reshape(SLOTS, columns), second.reshape(SLOTS, columns)


def session_bias(counts, offsets):
    def place(slot):
        block = lax.shift_right_logical(slot, BLOCK_SHIFT)
        start = jnp.zeros_like(slot)
        count = jnp.zeros_like(slot)
        for j in range(SESSIONS):
            reached = block >= offsets[0, j]
            start = jnp.where(reached, offsets[0, j], start)
            count = jnp.where(reached, counts[0, j], count)
        return start, count

    keys = lax.broadcasted_iota(jnp.int32, (SLOTS, LANES), 0)
    key_start, key_count = place(keys)
    live = keys - (1 << BLOCK_SHIFT) * key_start < key_count
    key_start = jnp.where(live, key_start, -1)
    halves = []
    for half in range(SLOTS // LANES):
        queries = lax.broadcasted_iota(jnp.int32, (SLOTS, LANES), 1) + half * LANES
        query_start, _ = place(queries)
        halves.append(jnp.where(query_start == key_start, 0.0, -1e30))
    return jnp.concatenate(halves, axis=1)


def kernel(
    counts,
    offsets,
    act,
    out_grad,
    table,
    layout,
    input_grad,
    table_grad,
    embedded,
    saved,
    bias,
    chosen,
    chosen_t,
    rows_in,
    rows_grad,
    rows_out,
    send_mix,
    recv_mix,
    send_back,
    recv_back,
    send_sum,
    recv_sum,
    send_group,
    recv_group,
    send_part,
    recv_part,
    mix_sems,
    back_sems,
    sum_sems,
    group_sems,
    part_sems,
):
    me = lax.axis_index("shard")
    group = lax.axis_index("group")

    barrier = pltpu.get_barrier_semaphore()

    @pl.loop(1, SHARDS)
    def _(step):
        peer = lax.rem(me + step, SHARDS)
        pl.semaphore_signal(barrier, inc=1, device_id=(group, peer), device_id_type=MESH)

    for step in range(1, GROUPS):
        other = lax.rem(group + step, GROUPS)
        pl.semaphore_signal(barrier, inc=1, device_id=(other, me), device_id_type=MESH)

    bias[...] = session_bias(counts, offsets)
    template = lax.broadcasted_iota(jnp.int32, (TEMPLATES, SLOTS), 0)
    hit = jnp.where(template == layout[...], 1.0, 0.0)
    chosen_t[...] = hit.astype(BF16)
    chosen[...] = jnp.transpose(hit).astype(BF16)

    def block_copy(source, target, sems, chunk, peer, slot):
        pairs = pl.ds(chunk * PER_CHUNK, PER_CHUNK)
        return pltpu.make_async_remote_copy(
            src_ref=source.at[pairs, peer],
            dst_ref=target.at[pairs, slot],
            send_sem=sems.at[0, chunk],
            recv_sem=sems.at[1, chunk],
            device_id=(group, peer),
            device_id_type=MESH,
        )

    def all_blocks(source, target, sems, chunk):
        pairs = pl.ds(chunk * PER_CHUNK, PER_CHUNK)
        others = pl.ds(0, SHARDS - 1)
        return pltpu.make_async_remote_copy(
            src_ref=source.at[pairs, others],
            dst_ref=target.at[pairs, others],
            send_sem=sems.at[0, chunk],
            recv_sem=sems.at[1, chunk],
            device_id=(group, lax.rem(me + 1, SHARDS)),
            device_id_type=MESH,
        )

    def send_chunk(source, target, sems, chunk):
        @pl.loop(1, SHARDS)
        def _(step):
            peer = lax.rem(me + step, SHARDS)
            block_copy(source, target, sems, chunk, peer, me).start()

        for pair in range(PER_CHUNK):
            at = chunk * PER_CHUNK + pair
            target[at, me] = source[at, me]

    def spatial_step(pair):
        lanes = pl.ds(pl.multiple_of(pair * LANES, LANES), LANES)
        rows = mm(chosen[...], table[:, lanes])
        mixed = []
        for patch in range(2):
            values = (act[0, patch, :, lanes].astype(F32) + rows).astype(BF16)
            embedded[patch, pair] = values
            out, weights = spatial_pair(values, bias[...])
            for head in range(2):
                saved[patch, pair, head] = weights[head]
            mixed.append(out)
        send_mix[pair] = weave(mixed[0], mixed[1], pltpu.roll).astype(BF16)

    def temporal_step(pair):
        lanes = pl.ds(pl.multiple_of(pair * LANES, LANES), LANES)
        rows_in[...] = recv_mix[pair].astype(F32).reshape(PATCHES * 4, LANES)
        rows_grad[:, 0:4, :] = out_grad[0, :, :, lanes].astype(F32)
        flat_grad = rows_grad.reshape(PATCHES * 8, LANES)
        for slot in range(4):
            values = rows_in[pl.ds(slot, PATCHES, stride=4), :].astype(BF16)
            cotangent = flat_grad[pl.ds(slot, PATCHES, stride=8), :].astype(BF16)
            rows_out[pl.ds(slot, PATCHES, stride=4), :] = temporal_pair(values, cotangent)
        send_back[pair] = rows_out[...].reshape(SHARDS, 8, LANES).astype(BF16)

    def back_step(pair):
        lanes = pl.ds(pl.multiple_of(pair * LANES, LANES), LANES)
        grads = unweave(recv_back[pair].astype(F32), pltpu.roll)
        electrode = None
        for patch in range(2):
            full = spatial_back_pair(
                embedded[patch, pair],
                [saved[patch, pair, head] for head in range(2)],
                grads[patch].astype(BF16),
            )
            input_grad[0, patch, :, lanes] = full.astype(BF16)
            electrode = full if electrode is None else electrode + full
        owners = LANES // OWN_COLS
        send_sum[pl.ds(pair * owners, owners)] = (
            jnp.transpose(electrode).astype(BF16).reshape(owners, OWN_COLS, SLOTS)
        )

    def over_pairs(chunk, step):
        @pl.loop(0, PER_CHUNK)
        def _(pair):
            step(chunk * PER_CHUNK + pair)

    over_pairs(0, spatial_step)
    pl.semaphore_wait(barrier, SHARDS - 1 + GROUPS - 1)
    send_chunk(send_mix, recv_mix, mix_sems, 0)

    @pl.loop(1, CHUNKS)
    def _(chunk):
        over_pairs(chunk, spatial_step)
        send_chunk(send_mix, recv_mix, mix_sems, chunk)

    @pl.loop(0, CHUNKS)
    def _(chunk):
        all_blocks(send_mix, recv_mix, mix_sems, chunk).wait_recv()
        over_pairs(chunk, temporal_step)
        send_chunk(send_back, recv_back, back_sems, chunk)

    @pl.loop(0, CHUNKS)
    def _(chunk):
        all_blocks(send_back, recv_back, back_sems, chunk).wait_recv()
        over_pairs(chunk, back_step)

    def to_shards(source_at, target, sems):
        @pl.loop(1, SHARDS)
        def _(step):
            peer = lax.rem(me + step, SHARDS)
            pltpu.make_async_remote_copy(
                src_ref=source_at(peer),
                dst_ref=target.at[me],
                send_sem=sems.at[0],
                recv_sem=sems.at[1],
                device_id=(group, peer),
                device_id_type=MESH,
            ).start()

    def from_shards(target, sems):
        others = pl.ds(0, SHARDS - 1)
        return pltpu.make_async_remote_copy(
            src_ref=target.at[others],
            dst_ref=target.at[others],
            send_sem=sems.at[0],
            recv_sem=sems.at[1],
            device_id=(group, lax.rem(me + 1, SHARDS)),
            device_id_type=MESH,
        )

    to_shards(lambda peer: send_sum.at[peer], recv_sum, sum_sems)
    recv_sum[me] = send_sum[me]
    from_shards(recv_sum, sum_sems).wait_recv()

    columns = jnp.zeros((OWN_COLS, SLOTS), F32)
    for part in range(8):
        columns = columns + jnp.sum(recv_sum[part * 8 : part * 8 + 8].astype(F32), axis=0)
    high = columns.astype(BF16)
    low = (columns - high.astype(F32)).astype(BF16)
    own = mm_nt(high, chosen_t[...]) + mm_nt(low, chosen_t[...])
    for other in range(GROUPS):
        send_group[other] = own[:, other * OWN_ROWS : (other + 1) * OWN_ROWS]
    copies = []
    for step in range(1, GROUPS):
        other = lax.rem(group + step, GROUPS)
        copy = pltpu.make_async_remote_copy(
            src_ref=send_group.at[other],
            dst_ref=recv_group.at[step],
            send_sem=group_sems.at[0, step],
            recv_sem=group_sems.at[1, step],
            device_id=(other, me),
            device_id_type=MESH,
        )
        copy.start()
        copies.append(copy)
    part = send_group[group]
    for step, copy in enumerate(copies):
        copy.wait_recv()
        part = part + recv_group[step + 1]
    part = part.astype(BF16)
    send_part[...] = part
    to_shards(lambda peer: send_part, recv_part, part_sems)
    recv_part[me] = part
    from_shards(recv_part, part_sems).wait_recv()
    turned = recv_part[...].astype(F32).reshape(WIDTH, OWN_ROWS)
    table_grad[...] = jnp.transpose(turned)

    @pl.loop(0, CHUNKS)
    def _(chunk):
        all_blocks(send_mix, recv_mix, mix_sems, chunk).wait_send()
        all_blocks(send_back, recv_back, back_sems, chunk).wait_send()

    from_shards(recv_sum, sum_sems).wait_send()
    from_shards(recv_part, part_sems).wait_send()
    for copy in copies:
        copy.wait_send()


def body(activations, out_grad, embedding, counts, offsets, layout):
    vmem = pl.BlockSpec(memory_space=pltpu.VMEM)
    smem = pl.BlockSpec(memory_space=pltpu.SMEM)
    scratch = [
        pltpu.VMEM((2, PAIRS, SLOTS, LANES), BF16),
        pltpu.VMEM((2, PAIRS, 2, SLOTS, SLOTS), BF16),
        pltpu.VMEM((SLOTS, SLOTS), F32),
        pltpu.VMEM((SLOTS, TEMPLATES), BF16),
        pltpu.VMEM((TEMPLATES, SLOTS), BF16),
        pltpu.VMEM((PATCHES * 4, LANES), F32),
        pltpu.VMEM((PATCHES, 8, LANES), F32),
        pltpu.VMEM((PATCHES * 4, LANES), F32),
        pltpu.VMEM((PAIRS, SHARDS, 8, LANES), BF16),
        pltpu.VMEM((PAIRS, SHARDS, 8, LANES), BF16),
        pltpu.VMEM((PAIRS, SHARDS, 8, LANES), BF16),
        pltpu.VMEM((PAIRS, SHARDS, 8, LANES), BF16),
        pltpu.VMEM((SHARDS, OWN_COLS, SLOTS), BF16),
        pltpu.VMEM((SHARDS, OWN_COLS, SLOTS), BF16),
        pltpu.VMEM((GROUPS, OWN_COLS, OWN_ROWS), F32),
        pltpu.VMEM((GROUPS, OWN_COLS, OWN_ROWS), F32),
        pltpu.VMEM((OWN_COLS, OWN_ROWS), BF16),
        pltpu.VMEM((SHARDS, OWN_COLS, OWN_ROWS), BF16),
        pltpu.SemaphoreType.DMA((2, CHUNKS)),
        pltpu.SemaphoreType.DMA((2, CHUNKS)),
        pltpu.SemaphoreType.DMA((2,)),
        pltpu.SemaphoreType.DMA((2, GROUPS)),
        pltpu.SemaphoreType.DMA((2,)),
    ]
    return pl.pallas_call(
        kernel,
        out_shape=(
            jax.ShapeDtypeStruct(activations.shape, BF16),
            jax.ShapeDtypeStruct((OWN_ROWS, WIDTH), F32),
        ),
        in_specs=[smem, smem, vmem, vmem, vmem, vmem],
        out_specs=(vmem, vmem),
        scratch_shapes=scratch,
        compiler_params=pltpu.CompilerParams(
            collective_id=0, has_side_effects=True, vmem_limit_bytes=60 << 20
        ),
    )(counts, offsets, activations, out_grad, embedding, layout)


def solution(mesh):
    placed = (
        P("group", "shard", None, None),
        P("group", None, "shard", None),
        P(),
        P("group", None),
        P("group", None),
        P("group", None),
    )
    return jax.shard_map(
        body,
        mesh=mesh,
        in_specs=placed,
        out_specs=(P("group", "shard", None, None), P("group", None)),
        check_vma=False,
    )
```

time: 441 us -> 98.4 us (0.22)
  waiting for transfers between devices: 311 us -> 0 us
  Pallas kernels: 0 us -> 94.5 us
  matrix products: 42.1 us -> 0 us
  local copies, waits for them, and re-layouts: 31.5 us -> 3.12 us
  other arithmetic: 21.3 us -> 0 us
  starting transfers between devices: 19.4 us -> 0 us
  between operations: 14.2 us -> 0.65 us
    psum x1 -> x0, waiting for transfers between devices: 257 us -> none  [body(): summed_table = lax.psum(local_table, ('group', 'shard'))]
    pallas_call x0 -> x1, Pallas kernels: none -> 94.5 us  [body(): pl.pallas_call(kernel, out_shape=(jax.ShapeDtypeStruct(activations.shape,...]
    all_to_all x2 -> x0, waiting for transfers between devices: 54.1 us -> none  [the longest x1 28.3 us: body(): lax.all_to_all(jnp.moveaxis(mixed_grad, 0, 1)[None], 'shard', split_axis=...]
    dot_general x34 -> x0, matrix products: 22.5 us -> none  [the longest x32 19.4 us: product(): return jnp.einsum(form, left, right, preferred_element_type=jnp.float32)]
    sub x8 -> x0, matrix products: 19.6 us -> none  [attend(): exponent = jnp.exp(scores - row_max)]
    all_to_all x2 -> x0, starting transfers between devices: 19.2 us -> none  [the longest x1 13 us: body(): lax.all_to_all(mixed[None], 'shard', split_axis=2, concat_axis=1, tiled=T...]
    while x4 -> x0, local copies, waits for them, and re-layouts: 11.7 us -> none  [the longest x2 5.38 us: body(): lax.map(temporal, (jnp.moveaxis(gathered[0], 1, 0), jnp.moveaxis(out_grad...]
    convert_element_type x7 -> x0, other arithmetic: 10.8 us -> none  [the longest x6 10.6 us: attend(): (exponent / jnp.sum(exponent, axis=-1, keepdims=True)).astype(jnp.bfloat16)]
  transfers between devices with their start and end apart: 3 -> 0, of which waited for: 3 -> 0; matrix products, arithmetic and copies ran while one was open for 1% -> 0% of each run, Pallas kernels for 0% -> 0%
where the time goes in v2:
time: 98.4 us; the launch traced here: 98.3 us
  Pallas kernels  94.5 us (96%)
  local copies, waits for them, and re-layouts  3.12 us (3%)
    pallas_call x1, Pallas kernels, body(): pl.pallas_call(kernel, out_shape=(jax.ShapeDtypeStruct(activations.shape,...  94.5 us
    unnamed x4, local copies, waits for them, and re-layouts  3.12 us

profile of v2, /device:TPU:1, one launch (start us, length us, event | category | flops | bytes accessed | tf_op | source)
XLA Modules:
  0.0 98.3 jit_solution(17159970976308257949)
XLA Ops:
  0.6 94.5 %shard_map.77 = (bf16[1,2,256,1024]{3,2,1,0:T(8,128)(2,1)}, f32[128,1024]{1,0:T(8,128)}) custom-call(s32[1,8]{1,0:T(1,128)} %counts.1, s32[1,8]{1,0:T(1,128)} %offsets.1, bf16[1,2,256,1024]{3,2,1,0:T(8,128)(2,1)} %act.1, bf16[1,128,4,1024]{3,2,1,0:T(4,128)(2,1)} %out_grad.1, bf16[512,1024]{1,0:T(8,128)(2,1)} %table.1, s32[1,256]{1,0:T(1,128)} %layout.1), custom_call_target="tpu_custom_call" | custom-call | tf_op jit(solution)/shard_map/pallas_call | solution.py:397
  95.1 0.0 copy-start
  95.2 2.3 %copy.10 = bf16[1,2,256,1024]{3,2,1,0:T(8,128)(2,1)} copy(bf16[1,2,256,1024]{3,2,1,0:T(8,128)(2,1)} %get-tuple-element.4) | data formatting | bytes 2097152
  97.5 0.0 copy-done
  97.5 0.8 copy.11
Async XLA Ops:
  95.1 2.3 %copy-start = (f32[128,1024]{1,0:T(8,128)S(1)}, f32[128,1024]{1,0:T(8,128)}, u32[]{:S(2)}) copy-start(f32[128,1024]{1,0:T(8,128)} %get-tuple-element.5) | copy-start | bytes 1572868

commit v3 on v2

--- a/solution.py
+++ b/solution.py
@@ -13,13 +13,13 @@
 HALF = 64
 LANES = 128
 PAIRS = 8
-CHUNKS = 4
-PER_CHUNK = PAIRS // CHUNKS
 SLOTS = 256
 PATCHES = 128
 TEMPLATES = 512
 WIDTH = 1024
-OWN_COLS = WIDTH // SHARDS
+CHIPS = SHARDS // 2
+STAGES = 2
+OWN_COLS = WIDTH // SHARDS // STAGES
 OWN_ROWS = TEMPLATES // GROUPS
 SCALE = 0.0625
 BLOCK_SHIFT = 5
@@ -145,17 +145,19 @@
 def kernel(
     counts,
     offsets,
+    act_hbm,
+    out_grad_hbm,
+    table_hbm,
+    layout,
+    input_grad,
+    table_grad,
     act,
     out_grad,
     table,
-    layout,
-    input_grad,
-    table_grad,
     embedded,
     saved,
     bias,
     chosen,
-    chosen_t,
     rows_in,
     rows_grad,
     rows_out,
@@ -163,20 +165,35 @@
     recv_mix,
     send_back,
     recv_back,
-    send_sum,
+    partial,
+    recv_pair,
+    summed,
     recv_sum,
     send_group,
     recv_group,
     send_part,
     recv_part,
+    load_sems,
     mix_sems,
     back_sems,
+    pair_sems,
     sum_sems,
     group_sems,
     part_sems,
 ):
     me = lax.axis_index("shard")
     group = lax.axis_index("group")
+    chip = me // 2
+    core = lax.rem(me, 2)
+    partner = me + 1 - 2 * core
+
+    loads = [
+        pltpu.make_async_copy(act_hbm, act, load_sems.at[0]),
+        pltpu.make_async_copy(table_hbm, table, load_sems.at[1]),
+        pltpu.make_async_copy(out_grad_hbm, out_grad, load_sems.at[2]),
+    ]
+    for load in loads:
+        load.start()
 
     barrier = pltpu.get_barrier_semaphore()
 
@@ -192,41 +209,31 @@
     bias[...] = session_bias(counts, offsets)
     template = lax.broadcasted_iota(jnp.int32, (TEMPLATES, SLOTS), 0)
     hit = jnp.where(template == layout[...], 1.0, 0.0)
-    chosen_t[...] = hit.astype(BF16)
     chosen[...] = jnp.transpose(hit).astype(BF16)
 
-    def block_copy(source, target, sems, chunk, peer, slot):
-        pairs = pl.ds(chunk * PER_CHUNK, PER_CHUNK)
+    def remote(source, target, sems, at, peer):
         return pltpu.make_async_remote_copy(
-            src_ref=source.at[pairs, peer],
-            dst_ref=target.at[pairs, slot],
-            send_sem=sems.at[0, chunk],
-            recv_sem=sems.at[1, chunk],
-            device_id=(group, peer),
+            src_ref=source,
+            dst_ref=target,
+            send_sem=sems.at[(0, *at)],
+            recv_sem=sems.at[(1, *at)],
+            device_id=peer,
             device_id_type=MESH,
         )
 
-    def all_blocks(source, target, sems, chunk):
-        pairs = pl.ds(chunk * PER_CHUNK, PER_CHUNK)
-        others = pl.ds(0, SHARDS - 1)
-        return pltpu.make_async_remote_copy(
-            src_ref=source.at[pairs, others],
-            dst_ref=target.at[pairs, others],
-            send_sem=sems.at[0, chunk],
-            recv_sem=sems.at[1, chunk],
-            device_id=(group, lax.rem(me + 1, SHARDS)),
-            device_id_type=MESH,
-        )
-
-    def send_chunk(source, target, sems, chunk):
+    def spread(source, target, sems, pair):
         @pl.loop(1, SHARDS)
         def _(step):
             peer = lax.rem(me + step, SHARDS)
-            block_copy(source, target, sems, chunk, peer, me).start()
-
-        for pair in range(PER_CHUNK):
-            at = chunk * PER_CHUNK + pair
-            target[at, me] = source[at, me]
+            remote(
+                source.at[pair, peer], target.at[pair, me], sems, (pair,), (group, peer)
+            ).start()
+
+        target[pair, me] = source[pair, me]
+
+    def several(buffer, count, sems, at):
+        whole = buffer.at[pl.ds(0, count)]
+        return remote(whole, whole, sems, at, (group, partner))
 
     def spatial_step(pair):
         lanes = pl.ds(pl.multiple_of(pair * LANES, LANES), LANES)
@@ -264,147 +271,202 @@
             )
             input_grad[0, patch, :, lanes] = full.astype(BF16)
             electrode = full if electrode is None else electrode + full
-        owners = LANES // OWN_COLS
-        send_sum[pl.ds(pair * owners, owners)] = (
-            jnp.transpose(electrode).astype(BF16).reshape(owners, OWN_COLS, SLOTS)
+        blocks = jnp.transpose(electrode).reshape(LANES // OWN_COLS, OWN_COLS, SLOTS)
+        partial[pair] = blocks.astype(BF16)
+
+    half = LANES // OWN_COLS
+
+    def exchange_cores(duo):
+        return remote(
+            partial.at[2 * duo + 1 - core],
+            recv_pair.at[duo],
+            pair_sems,
+            (duo,),
+            (group, partner),
         )
 
-    def over_pairs(chunk, step):
-        @pl.loop(0, PER_CHUNK)
-        def _(pair):
-            step(chunk * PER_CHUNK + pair)
-
-    over_pairs(0, spatial_step)
-    pl.semaphore_wait(barrier, SHARDS - 1 + GROUPS - 1)
-    send_chunk(send_mix, recv_mix, mix_sems, 0)
-
-    @pl.loop(1, CHUNKS)
-    def _(chunk):
-        over_pairs(chunk, spatial_step)
-        send_chunk(send_mix, recv_mix, mix_sems, chunk)
-
-    @pl.loop(0, CHUNKS)
-    def _(chunk):
-        all_blocks(send_mix, recv_mix, mix_sems, chunk).wait_recv()
-        over_pairs(chunk, temporal_step)
-        send_chunk(send_back, recv_back, back_sems, chunk)
-
-    @pl.loop(0, CHUNKS)
-    def _(chunk):
-        all_blocks(send_back, recv_back, back_sems, chunk).wait_recv()
-        over_pairs(chunk, back_step)
-
-    def to_shards(source_at, target, sems):
+    def sum_cores(stage):
+        for part in range(2):
+            duo = 2 * stage + part
+            exchange_cores(duo).wait_recv()
+            own = partial[2 * duo + core].astype(F32)
+            both = own + recv_pair[duo].astype(F32)
+            summed[stage, part * half : (part + 1) * half] = both.astype(BF16)
+
+        @pl.loop(1, CHIPS)
+        def _(step):
+            peer = lax.rem(chip + step, CHIPS)
+            remote(
+                summed.at[stage, peer],
+                recv_sum.at[stage, chip],
+                sum_sems,
+                (stage,),
+                (group, 2 * peer + core),
+            ).start()
+
+        recv_sum[stage, chip] = summed[stage, chip]
+
+    def group_copies(stage):
+        copies = []
+        for step in range(1, GROUPS):
+            other = lax.rem(group + step, GROUPS)
+            copies.append(
+                remote(
+                    send_group.at[stage, other],
+                    recv_group.at[stage, step],
+                    group_sems,
+                    (stage, step),
+                    (other, me),
+                )
+            )
+        return copies
+
+    def sum_chips(stage):
+        several(recv_sum.at[stage], CHIPS - 1, sum_sems, (stage,)).wait_recv()
+        columns = jnp.sum(recv_sum[stage].astype(F32), axis=0)
+        high = columns.astype(BF16)
+        low = (columns - high.astype(F32)).astype(BF16)
+        both = mm(jnp.concatenate([high, low], axis=0), chosen[...])
+        own = both[:OWN_COLS] + both[OWN_COLS:]
+        for other in range(GROUPS):
+            rows = own[:, other * OWN_ROWS : (other + 1) * OWN_ROWS]
+            send_group[stage, other] = rows
+        for copy in group_copies(stage):
+            copy.start()
+
+    def sum_groups(stage):
+        part = send_group[stage, group]
+        for step, copy in enumerate(group_copies(stage)):
+            copy.wait_recv()
+            part = part + recv_group[stage, step + 1]
+        part = part.astype(BF16)
+        send_part[stage] = part
+        slot = (2 * (chip // half) + core) * half + lax.rem(chip, half)
+
         @pl.loop(1, SHARDS)
         def _(step):
             peer = lax.rem(me + step, SHARDS)
-            pltpu.make_async_remote_copy(
-                src_ref=source_at(peer),
-                dst_ref=target.at[me],
-                send_sem=sems.at[0],
-                recv_sem=sems.at[1],
-                device_id=(group, peer),
-                device_id_type=MESH,
+            remote(
+                send_part.at[stage],
+                recv_part.at[stage, slot],
+                part_sems,
+                (stage,),
+                (group, peer),
             ).start()
 
-    def from_shards(target, sems):
-        others = pl.ds(0, SHARDS - 1)
-        return pltpu.make_async_remote_copy(
-            src_ref=target.at[others],
-            dst_ref=target.at[others],
-            send_sem=sems.at[0],
-            recv_sem=sems.at[1],
-            device_id=(group, lax.rem(me + 1, SHARDS)),
-            device_id_type=MESH,
-        )
-
-    to_shards(lambda peer: send_sum.at[peer], recv_sum, sum_sems)
-    recv_sum[me] = send_sum[me]
-    from_shards(recv_sum, sum_sems).wait_recv()
-
-    columns = jnp.zeros((OWN_COLS, SLOTS), F32)
-    for part in range(8):
-        columns = columns + jnp.sum(recv_sum[part * 8 : part * 8 + 8].astype(F32), axis=0)
-    high = columns.astype(BF16)
-    low = (columns - high.astype(F32)).astype(BF16)
-    own = mm_nt(high, chosen_t[...]) + mm_nt(low, chosen_t[...])
-    for other in range(GROUPS):
-        send_group[other] = own[:, other * OWN_ROWS : (other + 1) * OWN_ROWS]
-    copies = []
-    for step in range(1, GROUPS):
-        other = lax.rem(group + step, GROUPS)
-        copy = pltpu.make_async_remote_copy(
-            src_ref=send_group.at[other],
-            dst_ref=recv_group.at[step],
-            send_sem=group_sems.at[0, step],
-            recv_sem=group_sems.at[1, step],
-            device_id=(other, me),
-            device_id_type=MESH,
-        )
-        copy.start()
-        copies.append(copy)
-    part = send_group[group]
-    for step, copy in enumerate(copies):
-        copy.wait_recv()
-        part = part + recv_group[step + 1]
-    part = part.astype(BF16)
-    send_part[...] = part
-    to_shards(lambda peer: send_part, recv_part, part_sems)
-    recv_part[me] = part
-    from_shards(recv_part, part_sems).wait_recv()
-    turned = recv_part[...].astype(F32).reshape(WIDTH, OWN_ROWS)
-    table_grad[...] = jnp.transpose(turned)
-
-    @pl.loop(0, CHUNKS)
-    def _(chunk):
-        all_blocks(send_mix, recv_mix, mix_sems, chunk).wait_send()
-        all_blocks(send_back, recv_back, back_sems, chunk).wait_send()
-
-    from_shards(recv_sum, sum_sems).wait_send()
-    from_shards(recv_part, part_sems).wait_send()
-    for copy in copies:
-        copy.wait_send()
+        recv_part[stage, slot] = part
+
+    def write_table(stage):
+        several(recv_part.at[stage], SHARDS - 1, part_sems, (stage,)).wait_recv()
+        columns = WIDTH // STAGES
+        turned = recv_part[stage].astype(F32).reshape(columns, OWN_ROWS)
+        table_grad[:, stage * columns : (stage + 1) * columns] = jnp.transpose(turned)
+
+    loads[0].wait()
+    loads[1].wait()
+    spatial_step(0)
+    pl.semaphore_wait(barrier, SHARDS - 1 + GROUPS - 1)
+    spread(send_mix, recv_mix, mix_sems, 0)
+
+    @pl.loop(1, PAIRS)
+    def _(pair):
+        spatial_step(pair)
+        spread(send_mix, recv_mix, mix_sems, pair)
+
+    loads[2].wait()
+
+    @pl.loop(0, PAIRS)
+    def _(pair):
+        several(recv_mix.at[pair], SHARDS - 1, mix_sems, (pair,)).wait_recv()
+        temporal_step(pair)
+        spread(send_back, recv_back, back_sems, pair)
+
+    @pl.loop(0, PAIRS)
+    def _(pair):
+        several(recv_back.at[pair], SHARDS - 1, back_sems, (pair,)).wait_recv()
+        back_step(pair)
+
+        @pl.when(lax.rem(pair, 2) == 1)
+        def _():
+            exchange_cores(pair // 2).start()
+
+        @pl.when(pair == 4)
+        def _():
+            sum_cores(0)
+
+        @pl.when(pair == 6)
+        def _():
+            sum_chips(0)
+
+    sum_groups(0)
+    sum_cores(1)
+    write_table(0)
+    sum_chips(1)
+    sum_groups(1)
+    write_table(1)
+
+    @pl.loop(0, PAIRS)
+    def _(pair):
+        several(send_mix.at[pair], SHARDS - 1, mix_sems, (pair,)).wait_send()
+        several(send_back.at[pair], SHARDS - 1, back_sems, (pair,)).wait_send()
+
+    for duo in range(PAIRS // 2):
+        exchange_cores(duo).wait_send()
+    for stage in range(STAGES):
+        several(summed.at[stage], CHIPS - 1, sum_sems, (stage,)).wait_send()
+        several(recv_part.at[stage], SHARDS - 1, part_sems, (stage,)).wait_send()
+        for copy in group_copies(stage):
+            copy.wait_send()
 
 
 def body(activations, out_grad, embedding, counts, offsets, layout):
     vmem = pl.BlockSpec(memory_space=pltpu.VMEM)
     smem = pl.BlockSpec(memory_space=pltpu.SMEM)
+    hbm = pl.BlockSpec(memory_space=pltpu.HBM)
+    blocks = pltpu.VMEM((PAIRS, SHARDS, 8, LANES), BF16)
+    halves = LANES // OWN_COLS
     scratch = [
+        pltpu.VMEM(activations.shape, BF16),
+        pltpu.VMEM(out_grad.shape, BF16),
+        pltpu.VMEM(embedding.shape, BF16),
         pltpu.VMEM((2, PAIRS, SLOTS, LANES), BF16),
         pltpu.VMEM((2, PAIRS, 2, SLOTS, SLOTS), BF16),
         pltpu.VMEM((SLOTS, SLOTS), F32),
         pltpu.VMEM((SLOTS, TEMPLATES), BF16),
-        pltpu.VMEM((TEMPLATES, SLOTS), BF16),
         pltpu.VMEM((PATCHES * 4, LANES), F32),
         pltpu.VMEM((PATCHES, 8, LANES), F32),
         pltpu.VMEM((PATCHES * 4, LANES), F32),
-        pltpu.VMEM((PAIRS, SHARDS, 8, LANES), BF16),
-        pltpu.VMEM((PAIRS, SHARDS, 8, LANES), BF16),
-        pltpu.VMEM((PAIRS, SHARDS, 8, LANES), BF16),
-        pltpu.VMEM((PAIRS, SHARDS, 8, LANES), BF16),
-        pltpu.VMEM((SHARDS, OWN_COLS, SLOTS), BF16),
-        pltpu.VMEM((SHARDS, OWN_COLS, SLOTS), BF16),
-        pltpu.VMEM((GROUPS, OWN_COLS, OWN_ROWS), F32),
-        pltpu.VMEM((GROUPS, OWN_COLS, OWN_ROWS), F32),
-        pltpu.VMEM((OWN_COLS, OWN_ROWS), BF16),
-        pltpu.VMEM((SHARDS, OWN_COLS, OWN_ROWS), BF16),
-        pltpu.SemaphoreType.DMA((2, CHUNKS)),
-        pltpu.SemaphoreType.DMA((2, CHUNKS)),
-        pltpu.SemaphoreType.DMA((2,)),
-        pltpu.SemaphoreType.DMA((2, GROUPS)),
-        pltpu.SemaphoreType.DMA((2,)),
+        blocks,
+        blocks,
+        blocks,
+        blocks,
+        pltpu.VMEM((PAIRS, halves, OWN_COLS, SLOTS), BF16),
+        pltpu.VMEM((PAIRS // 2, halves, OWN_COLS, SLOTS), BF16),
+        pltpu.VMEM((STAGES, CHIPS, OWN_COLS, SLOTS), BF16),
+        pltpu.VMEM((STAGES, CHIPS, OWN_COLS, SLOTS), BF16),
+        pltpu.VMEM((STAGES, GROUPS, OWN_COLS, OWN_ROWS), F32),
+        pltpu.VMEM((STAGES, GROUPS, OWN_COLS, OWN_ROWS), F32),
+        pltpu.VMEM((STAGES, OWN_COLS, OWN_ROWS), BF16),
+        pltpu.VMEM((STAGES, SHARDS, OWN_COLS, OWN_ROWS), BF16),
+        pltpu.SemaphoreType.DMA((3,)),
+        pltpu.SemaphoreType.DMA((2, PAIRS)),
+        pltpu.SemaphoreType.DMA((2, PAIRS)),
+        pltpu.SemaphoreType.DMA((2, PAIRS // 2)),
+        pltpu.SemaphoreType.DMA((2, STAGES)),
+        pltpu.SemaphoreType.DMA((2, STAGES, GROUPS)),
+        pltpu.SemaphoreType.DMA((2, STAGES)),
     ]
     return pl.pallas_call(
         kernel,
         out_shape=(
-            jax.ShapeDtypeStruct(activations.shape, BF16),
-            jax.ShapeDtypeStruct((OWN_ROWS, WIDTH), F32),
+            pltpu.VMEM(activations.shape, BF16),
+            pltpu.VMEM((OWN_ROWS, WIDTH), F32),
         ),
-        in_specs=[smem, smem, vmem, vmem, vmem, vmem],
+        in_specs=[smem, smem, hbm, hbm, hbm, vmem],
         out_specs=(vmem, vmem),
         scratch_shapes=scratch,
         compiler_params=pltpu.CompilerParams(
-            collective_id=0, has_side_effects=True, vmem_limit_bytes=60 << 20
+            collective_id=0, has_side_effects=True, vmem_limit_bytes=56 << 20
         ),
     )(counts, offsets, activations, out_grad, embedding, layout)
 

time: 98.4 us -> 89.5 us (0.910)
  Pallas kernels: 94.5 us -> 87 us
  local copies, waits for them, and re-layouts: 3.12 us -> 1.77 us
    pallas_call x1, Pallas kernels: 94.5 us -> 87 us  [body(): pl.pallas_call(kernel, out_shape=(pltpu.VMEM(activations.shape, BF16), pl...]
    unnamed x4 -> x2, local copies, waits for them, and re-layouts: 3.12 us -> 1.77 us
where the time goes in v3:
time: 89.5 us; the launch traced here: 89.4 us
  Pallas kernels  87 us (97%)
  local copies, waits for them, and re-layouts  1.77 us (2%)
    pallas_call x1, Pallas kernels, body(): pl.pallas_call(kernel, out_shape=(pltpu.VMEM(activations.shape, BF16), pl...  87 us

profile of v3, /device:TPU:1, one launch (start us, length us, event | category | flops | bytes accessed | tf_op | source)
XLA Modules:
  0.0 89.4 jit_solution(5428894091135935785)
XLA Ops:
  0.6 87.0 %shard_map.77 = (bf16[1,2,256,1024]{3,2,1,0:T(8,128)(2,1)S(1)}, f32[128,1024]{1,0:T(8,128)S(1)}) custom-call(s32[1,8]{1,0:T(1,128)} %counts.1, s32[1,8]{1,0:T(1,128)} %offsets.1, bf16[1,2,256,1024]{3,2,1,0:T(8,128)(2,1)} %act_hbm.1, bf16[1,128,4,1024]{3,2,1,0:T(4,128)(2,1)} %out_grad_hbm.1, bf16[512,1024]{1,0:T(8,128)(2,1)} %table_hbm.1, s32[1,256]{1,0:T(1,128)} %layout.1), custom_call_target="tpu_custom_call" | custom-call | tf_op jit(solution)/shard_map/pallas_call | solution.py:459
  87.6 1.0 %copy.10 = bf16[1,2,256,1024]{3,2,1,0:T(8,128)(2,1)} copy(bf16[1,2,256,1024]{3,2,1,0:T(8,128)(2,1)S(1)} %get-tuple-element.2) | data formatting | bytes 2097152
  88.6 0.8 copy.11

commit v4 on v3

--- a/solution.py
+++ b/solution.py
@@ -17,9 +17,11 @@
 PATCHES = 128
 TEMPLATES = 512
 WIDTH = 1024
-CHIPS = SHARDS // 2
-STAGES = 2
-OWN_COLS = WIDTH // SHARDS // STAGES
+LINE = 8
+DEPTH = 8
+DUOS = PAIRS // 2
+SLICE = 32
+STAGES = ((0, 3), (3, 1))
 OWN_ROWS = TEMPLATES // GROUPS
 SCALE = 0.0625
 BLOCK_SHIFT = 5
@@ -166,26 +168,27 @@
     send_back,
     recv_back,
     partial,
-    recv_pair,
-    summed,
-    recv_sum,
+    recv_line,
     send_group,
     recv_group,
-    send_part,
-    recv_part,
+    send_depth,
+    recv_depth,
+    send_last,
+    recv_last,
     load_sems,
     mix_sems,
     back_sems,
-    pair_sems,
-    sum_sems,
+    line_sems,
     group_sems,
-    part_sems,
+    depth_sems,
+    last_sems,
 ):
     me = lax.axis_index("shard")
     group = lax.axis_index("group")
-    chip = me // 2
     core = lax.rem(me, 2)
-    partner = me + 1 - 2 * core
+    across = me // 16
+    deep = lax.rem(me // 2, DEPTH)
+    line = across * 2 + core
 
     loads = [
         pltpu.make_async_copy(act_hbm, act, load_sems.at[0]),
@@ -196,6 +199,9 @@
         load.start()
 
     barrier = pltpu.get_barrier_semaphore()
+
+    def beside(step):
+        return lax.rem(me + 16 * step, SHARDS)
 
     @pl.loop(1, SHARDS)
     def _(step):
@@ -224,7 +230,7 @@
     def spread(source, target, sems, pair):
         @pl.loop(1, SHARDS)
         def _(step):
-            peer = lax.rem(me + step, SHARDS)
+            peer = lax.rem(me + SHARDS - step, SHARDS)
             remote(
                 source.at[pair, peer], target.at[pair, me], sems, (pair,), (group, peer)
             ).start()
@@ -233,7 +239,7 @@
 
     def several(buffer, count, sems, at):
         whole = buffer.at[pl.ds(0, count)]
-        return remote(whole, whole, sems, at, (group, partner))
+        return remote(whole, whole, sems, at, (group, beside(1)))
 
     def spatial_step(pair):
         lanes = pl.ds(pl.multiple_of(pair * LANES, LANES), LANES)
@@ -271,99 +277,92 @@
             )
             input_grad[0, patch, :, lanes] = full.astype(BF16)
             electrode = full if electrode is None else electrode + full
-        blocks = jnp.transpose(electrode).reshape(LANES // OWN_COLS, OWN_COLS, SLOTS)
-        partial[pair] = blocks.astype(BF16)
-
-    half = LANES // OWN_COLS
-
-    def exchange_cores(duo):
-        return remote(
-            partial.at[2 * duo + 1 - core],
-            recv_pair.at[duo],
-            pair_sems,
-            (duo,),
-            (group, partner),
-        )
-
-    def sum_cores(stage):
-        for part in range(2):
-            duo = 2 * stage + part
-            exchange_cores(duo).wait_recv()
-            own = partial[2 * duo + core].astype(F32)
-            both = own + recv_pair[duo].astype(F32)
-            summed[stage, part * half : (part + 1) * half] = both.astype(BF16)
-
-        @pl.loop(1, CHIPS)
-        def _(step):
-            peer = lax.rem(chip + step, CHIPS)
-            remote(
-                summed.at[stage, peer],
-                recv_sum.at[stage, chip],
-                sum_sems,
-                (stage,),
-                (group, 2 * peer + core),
-            ).start()
-
-        recv_sum[stage, chip] = summed[stage, chip]
+        turned = jnp.transpose(electrode).astype(BF16)
+        partial[pair] = turned.reshape(LANES // SLICE, SLICE, SLOTS)
+
+    def on_line(step):
+        other = lax.rem(line + step, LINE)
+        return other, (group, (other // 2) * 16 + deep * 2 + lax.rem(other, 2))
+
+    def send_line(duo):
+        for step in range(1, LINE):
+            other, peer = on_line(step)
+            block = partial.at[2 * duo + lax.rem(other, 2), other // 2]
+            remote(block, recv_line.at[duo, line], line_sems, (duo,), peer).start()
+        recv_line[duo, line] = partial[2 * duo + core, across]
 
     def group_copies(stage):
+        first, count = STAGES[stage]
+        span = pl.ds(first, count)
         copies = []
         for step in range(1, GROUPS):
             other = lax.rem(group + step, GROUPS)
-            copies.append(
-                remote(
-                    send_group.at[stage, other],
-                    recv_group.at[stage, step],
-                    group_sems,
-                    (stage, step),
-                    (other, me),
-                )
-            )
+            source, target = send_group.at[other, span], recv_group.at[step, span]
+            copies.append(remote(source, target, group_sems, (stage, step), (other, me)))
         return copies
 
-    def sum_chips(stage):
-        several(recv_sum.at[stage], CHIPS - 1, sum_sems, (stage,)).wait_recv()
-        columns = jnp.sum(recv_sum[stage].astype(F32), axis=0)
-        high = columns.astype(BF16)
-        low = (columns - high.astype(F32)).astype(BF16)
-        both = mm(jnp.concatenate([high, low], axis=0), chosen[...])
-        own = both[:OWN_COLS] + both[OWN_COLS:]
+    def sum_line(stage):
+        first, count = STAGES[stage]
+        highs, lows = [], []
+        for duo in range(first, first + count):
+            several(recv_line.at[duo], LINE - 1, line_sems, (duo,)).wait_recv()
+            columns = jnp.sum(recv_line[duo].astype(F32), axis=0)
+            high = columns.astype(BF16)
+            highs.append(high)
+            lows.append((columns - high.astype(F32)).astype(BF16))
+        both = mm(jnp.concatenate(highs + lows, axis=0), chosen[...])
+        own = (both[: count * SLICE] + both[count * SLICE :]).astype(BF16)
         for other in range(GROUPS):
             rows = own[:, other * OWN_ROWS : (other + 1) * OWN_ROWS]
-            send_group[stage, other] = rows
+            send_group[other, first : first + count] = rows.reshape(count, SLICE, OWN_ROWS)
         for copy in group_copies(stage):
             copy.start()
 
     def sum_groups(stage):
-        part = send_group[stage, group]
+        first, count = STAGES[stage]
+        span = pl.ds(first, count)
+        part = send_group[group, span].astype(F32)
         for step, copy in enumerate(group_copies(stage)):
             copy.wait_recv()
-            part = part + recv_group[stage, step + 1]
-        part = part.astype(BF16)
-        send_part[stage] = part
-        slot = (2 * (chip // half) + core) * half + lax.rem(chip, half)
-
-        @pl.loop(1, SHARDS)
-        def _(step):
-            peer = lax.rem(me + step, SHARDS)
-            remote(
-                send_part.at[stage],
-                recv_part.at[stage, slot],
-                part_sems,
-                (stage,),
-                (group, peer),
-            ).start()
-
-        recv_part[stage, slot] = part
+            part = part + recv_group[step + 1, span].astype(F32)
+        send_depth[span] = part.astype(BF16)
+        for step in range(1, DEPTH):
+            peer = (group, across * 16 + lax.rem(deep + step, DEPTH) * 2 + core)
+            target = recv_depth.at[deep, span]
+            remote(send_depth.at[span], target, depth_sems, (stage,), peer).start()
+        recv_depth[deep, span] = part.astype(BF16)
+
+    def wide(buffer, stage):
+        first, count = STAGES[stage]
+        return buffer.at[:, pl.ds(first, count)]
+
+    def sum_depth(stage):
+        first, count = STAGES[stage]
+        span = pl.ds(first, count)
+        several(wide(recv_depth, stage), DEPTH - 1, depth_sems, (stage,)).wait_recv()
+        total = recv_depth[0, span].astype(F32)
+        for other in range(1, DEPTH):
+            total = total + recv_depth[other, span].astype(F32)
+        send_last[span] = total.astype(BF16)
+        for step in range(1, LINE):
+            _, peer = on_line(step)
+            target = recv_last.at[line, span]
+            remote(send_last.at[span], target, last_sems, (stage,), peer).start()
+        recv_last[line, span] = total.astype(BF16)
 
     def write_table(stage):
-        several(recv_part.at[stage], SHARDS - 1, part_sems, (stage,)).wait_recv()
-        columns = WIDTH // STAGES
-        turned = recv_part[stage].astype(F32).reshape(columns, OWN_ROWS)
-        table_grad[:, stage * columns : (stage + 1) * columns] = jnp.transpose(turned)
+        first, count = STAGES[stage]
+        several(wide(recv_last, stage), LINE - 1, last_sems, (stage,)).wait_recv()
+        for duo in range(first, first + count):
+            for side in range(2):
+                parts = [recv_last[2 * k + side, duo] for k in range(LANES // SLICE)]
+                turned = jnp.transpose(jnp.concatenate(parts, axis=0).astype(F32))
+                start = (2 * duo + side) * LANES
+                table_grad[:, start : start + LANES] = turned
 
     loads[0].wait()
     loads[1].wait()
+
     spatial_step(0)
     pl.semaphore_wait(barrier, SHARDS - 1 + GROUPS - 1)
     spread(send_mix, recv_mix, mix_sems, 0)
@@ -388,21 +387,18 @@
 
         @pl.when(lax.rem(pair, 2) == 1)
         def _():
-            exchange_cores(pair // 2).start()
-
-        @pl.when(pair == 4)
-        def _():
-            sum_cores(0)
+            send_line(pair // 2)
 
         @pl.when(pair == 6)
         def _():
-            sum_chips(0)
+            sum_line(0)
 
     sum_groups(0)
-    sum_cores(1)
+    sum_line(1)
+    sum_groups(1)
+    sum_depth(0)
+    sum_depth(1)
     write_table(0)
-    sum_chips(1)
-    sum_groups(1)
     write_table(1)
 
     @pl.loop(0, PAIRS)
@@ -410,11 +406,11 @@
         several(send_mix.at[pair], SHARDS - 1, mix_sems, (pair,)).wait_send()
         several(send_back.at[pair], SHARDS - 1, back_sems, (pair,)).wait_send()
 
-    for duo in range(PAIRS // 2):
-        exchange_cores(duo).wait_send()
-    for stage in range(STAGES):
-        several(summed.at[stage], CHIPS - 1, sum_sems, (stage,)).wait_send()
-        several(recv_part.at[stage], SHARDS - 1, part_sems, (stage,)).wait_send()
+    for duo in range(DUOS):
+        several(recv_line.at[duo], LINE - 1, line_sems, (duo,)).wait_send()
+    for stage in range(len(STAGES)):
+        several(wide(recv_depth, stage), DEPTH - 1, depth_sems, (stage,)).wait_send()
+        several(wide(recv_last, stage), LINE - 1, last_sems, (stage,)).wait_send()
         for copy in group_copies(stage):
             copy.wait_send()
 
@@ -424,7 +420,8 @@
     smem = pl.BlockSpec(memory_space=pltpu.SMEM)
     hbm = pl.BlockSpec(memory_space=pltpu.HBM)
     blocks = pltpu.VMEM((PAIRS, SHARDS, 8, LANES), BF16)
-    halves = LANES // OWN_COLS
+    slices = LANES // SLICE
+    rows = (DUOS, SLICE, OWN_ROWS)
     scratch = [
         pltpu.VMEM(activations.shape, BF16),
         pltpu.VMEM(out_grad.shape, BF16),
@@ -440,21 +437,21 @@
         blocks,
         blocks,
         blocks,
-        pltpu.VMEM((PAIRS, halves, OWN_COLS, SLOTS), BF16),
-        pltpu.VMEM((PAIRS // 2, halves, OWN_COLS, SLOTS), BF16),
-        pltpu.VMEM((STAGES, CHIPS, OWN_COLS, SLOTS), BF16),
-        pltpu.VMEM((STAGES, CHIPS, OWN_COLS, SLOTS), BF16),
-        pltpu.VMEM((STAGES, GROUPS, OWN_COLS, OWN_ROWS), F32),
-        pltpu.VMEM((STAGES, GROUPS, OWN_COLS, OWN_ROWS), F32),
-        pltpu.VMEM((STAGES, OWN_COLS, OWN_ROWS), BF16),
-        pltpu.VMEM((STAGES, SHARDS, OWN_COLS, OWN_ROWS), BF16),
+        pltpu.VMEM((PAIRS, slices, SLICE, SLOTS), BF16),
+        pltpu.VMEM((DUOS, LINE, SLICE, SLOTS), BF16),
+        pltpu.VMEM((GROUPS, *rows), BF16),
+        pltpu.VMEM((GROUPS, *rows), BF16),
+        pltpu.VMEM(rows, BF16),
+        pltpu.VMEM((DEPTH, *rows), BF16),
+        pltpu.VMEM(rows, BF16),
+        pltpu.VMEM((LINE, *rows), BF16),
         pltpu.SemaphoreType.DMA((3,)),
         pltpu.SemaphoreType.DMA((2, PAIRS)),
         pltpu.SemaphoreType.DMA((2, PAIRS)),
-        pltpu.SemaphoreType.DMA((2, PAIRS // 2)),
-        pltpu.SemaphoreType.DMA((2, STAGES)),
-        pltpu.SemaphoreType.DMA((2, STAGES, GROUPS)),
-        pltpu.SemaphoreType.DMA((2, STAGES)),
+        pltpu.SemaphoreType.DMA((2, DUOS)),
+        pltpu.SemaphoreType.DMA((2, len(STAGES), GROUPS)),
+        pltpu.SemaphoreType.DMA((2, len(STAGES))),
+        pltpu.SemaphoreType.DMA((2, len(STAGES))),
     ]
     return pl.pallas_call(
         kernel,

time: 89.5 us -> 83.3 us (0.931)
  Pallas kernels: 87 us -> 80.8 us
    pallas_call x1, Pallas kernels: 87 us -> 80.8 us  [body(): pl.pallas_call(kernel, out_shape=(pltpu.VMEM(activations.shape, BF16), pl...]
where the time goes in v4:
time: 83.3 us; the launch traced here: 83.2 us
  Pallas kernels  80.8 us (97%)
  local copies, waits for them, and re-layouts  1.77 us (2%)
    pallas_call x1, Pallas kernels, body(): pl.pallas_call(kernel, out_shape=(pltpu.VMEM(activations.shape, BF16), pl...  80.8 us
    unnamed x2, local copies, waits for them, and re-layouts  1.77 us

profile of v4, /device:TPU:1, one launch (start us, length us, event | category | flops | bytes accessed | tf_op | source)
XLA Modules:
  0.0 83.2 jit_solution(13680698164083721010)
XLA Ops:
  0.6 80.8 %shard_map.77 = (bf16[1,2,256,1024]{3,2,1,0:T(8,128)(2,1)S(1)}, f32[128,1024]{1,0:T(8,128)S(1)}) custom-call(s32[1,8]{1,0:T(1,128)} %counts.1, s32[1,8]{1,0:T(1,128)} %offsets.1, bf16[1,2,256,1024]{3,2,1,0:T(8,128)(2,1)} %act_hbm.1, bf16[1,128,4,1024]{3,2,1,0:T(4,128)(2,1)} %out_grad_hbm.1, bf16[512,1024]{1,0:T(8,128)(2,1)} %table_hbm.1, s32[1,256]{1,0:T(1,128)} %layout.1), custom_call_target="tpu_custom_call" | custom-call | tf_op jit(solution)/shard_map/pallas_call | solution.py:456
  81.5 1.0 %copy.10 = bf16[1,2,256,1024]{3,2,1,0:T(8,128)(2,1)} copy(bf16[1,2,256,1024]{3,2,1,0:T(8,128)(2,1)S(1)} %get-tuple-element.2) | data formatting | bytes 2097152
  82.4 0.8 copy.11

commit v5 on v4

--- a/solution.py
+++ b/solution.py
@@ -389,12 +389,9 @@
         def _():
             send_line(pair // 2)
 
-        @pl.when(pair == 6)
-        def _():
-            sum_line(0)
-
+    sum_line(0)
+    sum_line(1)
     sum_groups(0)
-    sum_line(1)
     sum_groups(1)
     sum_depth(0)
     sum_depth(1)

time: 83.3 us -> 82.9 us (level)
  no operation moved by 1% of the time
where the time goes in v5:
time: 82.9 us; the launch traced here: 82.8 us
  Pallas kernels  80.4 us (97%)
  local copies, waits for them, and re-layouts  1.77 us (2%)
    pallas_call x1, Pallas kernels, body(): pl.pallas_call(kernel, out_shape=(pltpu.VMEM(activations.shape, BF16), pl...  80.4 us
    unnamed x2, local copies, waits for them, and re-layouts  1.77 us

profile of v5, /device:TPU:1, one launch (start us, length us, event | category | flops | bytes accessed | tf_op | source)
XLA Modules:
  0.0 82.8 jit_solution(12266626779023848573)
XLA Ops:
  0.6 80.4 %shard_map.77 = (bf16[1,2,256,1024]{3,2,1,0:T(8,128)(2,1)S(1)}, f32[128,1024]{1,0:T(8,128)S(1)}) custom-call(s32[1,8]{1,0:T(1,128)} %counts.1, s32[1,8]{1,0:T(1,128)} %offsets.1, bf16[1,2,256,1024]{3,2,1,0:T(8,128)(2,1)} %act_hbm.1, bf16[1,128,4,1024]{3,2,1,0:T(4,128)(2,1)} %out_grad_hbm.1, bf16[512,1024]{1,0:T(8,128)(2,1)} %table_hbm.1, s32[1,256]{1,0:T(1,128)} %layout.1), custom_call_target="tpu_custom_call" | custom-call | tf_op jit(solution)/shard_map/pallas_call | solution.py:453
  81.0 1.0 %copy.10 = bf16[1,2,256,1024]{3,2,1,0:T(8,128)(2,1)} copy(bf16[1,2,256,1024]{3,2,1,0:T(8,128)(2,1)S(1)} %get-tuple-element.2) | data formatting | bytes 2097152
  82.0 0.8 copy.11
